TPU v7x, 512 devices: a whole 4x4x16 slice. The times are simulated.
512 devices in a mesh: slab: 128 (over y, z, core), sub: 4 (over x).
Axes of the slice: x: 4, y: 4, z: 16, core: 2. Of those that a mesh axis runs over, the one named last changes fastest.
Arguments:
- mode_shapes: bfloat16 [32, 6, 1024, 512], P(None, None, 'slab', 'sub')
- span_stiff: float32 [6, 1024, 512], P(None, 'slab', 'sub'), may hold values from -4 to 4
- chord_stiff: float32 [6, 1024, 512], P(None, 'slab', 'sub'), may hold values from -4 to 4
- span_geo: float32 [1024, 512], P('slab', 'sub'), may hold values from 0.2 to 2
- chord_geo: float32 [1024, 512], P('slab', 'sub'), may hold values from 0.2 to 2
- ground: float32 [6, 1024, 512], P(None, 'slab', 'sub'), may hold values from 0.2 to 2
- chord_len: int32 [1024], replicated, may hold values from 192 to 512, as said below
Outputs:
- adjoint: float32 [32, 6, 1024, 512], P(None, None, 'slab', 'sub')
- residual: float32 [32, 6, 1024, 512], P(None, None, 'slab', 'sub')
Inputs may be any that keep to these rules, and one draw needn't show every extreme that they name: chord_len[0] = 512.
All inputs are finite; a program needn't handle non-finite values.
Results may differ from a plain program's by a relative error of at most 0.0003.
Values sent between devices are 32-bit elements; how exact they have to be, the bound alone decides.
A program may use at most 64 MiB of HBM per device.

v0:
```python
import jax
import jax.numpy as jnp
from jax import lax
from jax.sharding import PartitionSpec as P

ITERS = 2


def from_behind(value, axis, steps):
    count = lax.axis_size(axis)
    initial, last = (max(0, -steps), min(count, count - steps))
    return lax.ppermute(value, axis, [(source, source + steps) for source in range(initial, last)])


def factor_blocks(blocks):
    count = len(blocks)
    factor = [[None] * count for i in range(count)]
    inverse = [None] * count
    for j in range(count):
        running = blocks[j][j]
        for k in range(j):
            running = running - factor[j][k] * factor[j][k]
        diag_root = jnp.sqrt(running)
        factor[j][j] = diag_root
        inverse[j] = 1.0 / diag_root
        for i in range(j + 1, count):
            running = blocks[i][j]
            for k in range(j):
                running = running - factor[i][k] * factor[j][k]
            factor[i][j] = running * inverse[j]
    return (factor, inverse)


def solve_blocks(factor, inverse, vector):
    count = len(inverse)
    forward = []
    for i in range(count):
        running = vector[:, i]
        for j in range(i):
            running = running - factor[i][j][None] * forward[j]
        forward.append(running * inverse[i][None])
    backward = [None] * count
    for i in reversed(range(count)):
        running = forward[i]
        for j in range(i + 1, count):
            running = running - factor[j][i][None] * backward[j]
        backward[i] = running * inverse[i][None]
    return jnp.stack(backward, axis=1)


def neighbours_ahead(field):
    next_station = from_behind(field[:, :, :1, :], "slab", -1)
    next_column = from_behind(field[:, :, :, :1], "sub", -1)
    span_next = jnp.concatenate([field[:, :, 1:, :], next_station], axis=2)
    chord_next = jnp.concatenate([field[:, :, :, 1:], next_column], axis=3)
    return (span_next, chord_next)


def forces_behind(span_forces, chord_forces):
    from_span = from_behind(span_forces[:, :, -1:, :], "slab", 1)
    from_chord = from_behind(chord_forces[:, :, :, -1:], "sub", 1)
    span_part = jnp.concatenate([from_span, span_forces[:, :, :-1, :]], axis=2)
    chord_part = jnp.concatenate([from_chord, chord_forces[:, :, :, :-1]], axis=3)
    return span_part + chord_part


def edge_forces(stiffness, jump, live_mask):
    strain = jnp.sum(stiffness[None] * jump, axis=1) * live_mask[None]
    return stiffness[None] * strain[:, None]


def operate_sent(field, span_stiff, chord_stiff, span_live, chord_live, ground):
    span_next, chord_next = neighbours_ahead(field)
    span_forces = edge_forces(span_stiff, span_next - field, span_live)
    chord_forces = edge_forces(chord_stiff, chord_next - field, chord_live)
    return (
        ground[None] * field - span_forces - chord_forces + forces_behind(span_forces, chord_forces)
    )


def inner_rz(first, second):
    return lax.psum(jnp.sum(first * second, axis=(1, 2, 3)), ("slab", "sub"))


def inner_pq(first, second):
    return lax.psum(jnp.sum(first * second, axis=(1, 2, 3)), ("slab", "sub"))


def body(mode_shapes, span_stiff, chord_stiff, span_geo, chord_geo, ground, chord_len):
    count = ground.shape[0]
    stations = ground.shape[1]
    columns = ground.shape[2]
    row_start = lax.axis_index("slab") * stations
    col_start = lax.axis_index("sub") * columns
    padded_len = jnp.concatenate(
        [jnp.zeros((1,), jnp.int32), chord_len, jnp.zeros((2,), jnp.int32)]
    )
    window = lax.dynamic_slice_in_dim(padded_len, row_start, stations + 2)
    col_global = (col_start + jnp.arange(columns, dtype=jnp.int32))[None, :]
    span_mask_wide = ((col_global < window[:-1, None]) & (col_global < window[1:, None])).astype(
        jnp.float32
    )
    col_wide = (col_start - 1 + jnp.arange(columns + 1, dtype=jnp.int32))[None, :]
    own_len = window[1 : stations + 1, None]
    chord_mask_wide = ((col_wide + 1 < own_len) & (col_wide >= 0)).astype(jnp.float32)
    span_live = span_mask_wide[1:]
    chord_live = chord_mask_wide[:, 1:]
    ghost_span = from_behind(span_stiff[:, stations - 1 :, :], "slab", 1)
    ghost_chord = from_behind(chord_stiff[:, :, columns - 1 :], "sub", 1)
    span_wide = jnp.concatenate([ghost_span, span_stiff], axis=1)
    chord_wide = jnp.concatenate([ghost_chord, chord_stiff], axis=2)
    blocks = []
    for i in range(count):
        block_row = []
        for j in range(count):
            span_pair = span_wide[i] * span_wide[j] * span_mask_wide
            chord_pair = chord_wide[i] * chord_wide[j] * chord_mask_wide
            entry = span_pair[1:] + span_pair[:-1] + chord_pair[:, 1:] + chord_pair[:, :-1]
            if i == j:
                entry = entry + ground[i]
            block_row.append(entry)
        blocks.append(block_row)
    factor, inverse = factor_blocks(blocks)
    mode_field = mode_shapes.astype(jnp.float32)
    span_next, chord_next = neighbours_ahead(mode_field)
    span_jump = span_next - mode_field
    chord_jump = chord_next - mode_field
    span_weight = jnp.sum(span_jump * span_jump, axis=1) * (span_geo * span_live)[None]
    chord_weight = jnp.sum(chord_jump * chord_jump, axis=1) * (chord_geo * chord_live)[None]
    span_load = span_stiff[None] * span_weight[:, None]
    chord_load = chord_stiff[None] * chord_weight[:, None]
    load = forces_behind(span_load, chord_load) - span_load - chord_load
    solution = jnp.zeros_like(load)
    residual = load
    precond = solve_blocks(factor, inverse, residual)
    direction = precond
    precond_norm = inner_rz(residual, precond)
    for step in range(ITERS):
        image = operate_sent(direction, span_stiff, chord_stiff, span_live, chord_live, ground)
        step_size = precond_norm / inner_pq(direction, image)
        solution = solution + step_size[:, None, None, None] * direction
        residual = residual - step_size[:, None, None, None] * image
        if step + 1 < ITERS:
            precond = solve_blocks(factor, inverse, residual)
            norm_next = inner_rz(residual, precond)
            direction = precond + (norm_next / precond_norm)[:, None, None, None] * direction
            precond_norm = norm_next
    return (solution, residual)


def solution(mesh):
    return jax.shard_map(
        body,
        mesh=mesh,
        in_specs=(
            P(None, None, "slab", "sub"),
            P(None, "slab", "sub"),
            P(None, "slab", "sub"),
            P("slab", "sub"),
            P("slab", "sub"),
            P(None, "slab", "sub"),
            P(),
        ),
        out_specs=(P(None, None, "slab", "sub"), P(None, None, "slab", "sub")),
        check_vma=False,
    )
```

profile of v0, /device:TPU:1, one launch (start us, length us, event | category | flops | bytes accessed | tf_op | source)
XLA Modules:
  0.0 413.0 jit_solution(10485907390977975643)
XLA Ops:
  0.6 0.7 slice.527
  1.4 4.9 %collective-permute-start.4 = (f32[6,1,128]{2,1,0:T(1,128)S(1)}, f32[6,1,128]{2,1,0:T(1,128)S(1)}, u32[]{:S(2)}, u32[]{:S(2)}) collective-permute-start(f32[6,1,128]{2,1,0:T(1,128)S(1)} %slice.527), channel_id=1, source_target_pairs={{0,4},{4,8},{8,12},{12,16},{16,20},{20,24},{24,28},{28,32},{32,36}... | collective-permute-start | bytes 9224 | tf_op jit(solution)/shard_map/ppermute | solution.py:12
  6.3 0.8 slice.531
  7.1 3.1 collective-permute-start.5
  10.2 1.1 copy_convert_fusion
  11.7 1.3 collective-permute-start.2
  13.0 3.3 collective-permute-start
  16.4 0.7 copy-done.25
  17.4 0.5 copy-done.26
  17.9 0.7 slice_select_fusion
  18.6 0.6 copy-done.27
  19.3 0.6 slice_select_fusion.1
  19.9 0.7 slice_convert_fusion
  20.9 0.5 copy-done.3
  21.6 0.6 copy-done.4
  22.5 0.7 copy-done.6
  23.4 0.7 fusion.94
  24.1 0.7 fusion.78
  24.7 0.6 copy-done.19
  25.3 0.7 fusion.70
  26.4 0.6 copy-done.5
  27.8 2.2 collective-permute-start.1
  30.8 4.0 collective-permute-start.3
  34.9 0.9 collective-permute-done.3
  36.2 1.3 fusion.3
  37.5 0.6 copy-done.13
  39.2 1.3 collective-permute-start.7
  40.5 3.8 collective-permute-start.6
  44.4 0.9 slice.780
  45.9 0.8 collective-permute-done.6
  46.7 1.6 fusion.9
  48.4 0.7 slice.784
  49.1 2.1 collective-permute-start.8
  51.3 1.2 slice.786
  52.5 2.1 copy.16
  54.6 4.4 %collective-permute-start.9 = (f32[32,6,8,1]{0,2,3,1:T(8,128)}, f32[32,6,8,1]{0,2,3,1:T(8,128)}, u32[]{:S(2)}, u32[]{:S(2)}) collective-permute-start(f32[32,6,8,1]{0,2,3,1:T(8,128)} %copy.16), channel_id=1, source_target_pairs={{0,1},{1,2},{2,3},{4,5},{5,6},{6,7},{8,9},{9,10},{10,11},{12,13},{... | collective-permute-start | bytes 18440 | tf_op jit(solution)/shard_map/ppermute | solution.py:12
  59.0 0.5 collective-permute-done.9
  59.5 2.0 copy.17
  61.5 2.6 multiply_reduce_fusion.2
  64.1 112.9 %all-reduce = (f32[32]{0:T(128)S(1)}, f32[32]{0:T(128)S(1)}) all-reduce(f32[32]{0:T(128)S(1)} %get-tuple-element.7, f32[32]{0:T(128)S(1)} %get-tuple-element.6), channel_id=1, replica_groups=mesh['slab'=128,'sub'=4] {'slab','sub'}, use_global_device_ids=true, to_apply=%region_3.0 | all-reduce | flops 64 | bytes 512 | tf_op jit(solution)/shard_map/psum | solution.py:82
  177.0 0.6 copy-done.28
  177.6 1.3 multiply_subtract_fusion.1
  179.0 0.4 multiply_dynamic-update-slice_fusion
  180.0 98.7 %psum.30 = f32[32]{0:T(128)S(1)} all-reduce(f32[32]{0:T(128)S(1)} %multiply_reduce_fusion.1), channel_id=1, replica_groups=mesh['slab'=128,'sub'=4] {'slab','sub'}, use_global_device_ids=true, to_apply=%region_9.0 | all-reduce | flops 32 | bytes 256 | tf_op jit(solution)/shard_map/psum | solution.py:82
  278.9 2.6 collective-permute-start.10
  281.8 1.3 collective-permute-start.11
  283.1 0.9 slice.794
  284.3 2.3 collective-permute-done.11
  286.6 1.2 copy.19
  287.9 1.8 fusion.14
  289.7 0.6 copy-done.18
  290.5 0.7 slice.798
  291.4 4.5 %collective-permute-start.12 = (f32[32,6,1,128]{3,0,2,1:T(8,128)}, f32[32,6,1,128]{3,0,2,1:T(8,128)}, u32[]{:S(2)}, u32[]{:S(2)}) collective-permute-start(f32[32,6,1,128]{3,0,2,1:T(8,128)} %slice.798), channel_id=1, source_target_pairs={{0,4},{4,8},{8,12},{12,16},{16,20},{20,24},{24,28},{28,32},{32,36}... | collective-permute-start | bytes 294920 | tf_op jit(solution)/shard_map/ppermute | solution.py:12
  296.0 1.2 slice.800
  297.1 1.5 copy.20
  298.6 2.9 collective-permute-start.13
  301.5 2.0 slice.799
  303.5 1.2 copy.21
  304.7 2.7 multiply_reduce_fusion
  307.5 100.6 %psum.31 = f32[32]{0:T(128)S(1)} all-reduce(f32[32]{0:T(128)S(1)} %get-tuple-element.14), channel_id=1, replica_groups=mesh['slab'=128,'sub'=4] {'slab','sub'}, use_global_device_ids=true, to_apply=%region_13.0 | all-reduce | flops 32 | bytes 256 | tf_op jit(solution)/shard_map/psum | solution.py:86
  408.1 0.7 copy-done.29
  408.8 1.5 multiply_subtract_fusion
  410.3 1.3 copy.23
  411.7 1.3 copy.22
  (127 shorter events, 7.9 us)
Async XLA Ops:
  1.4 20.2 %collective-permute-start.4 = (f32[6,1,128]{2,1,0:T(1,128)S(1)}, f32[6,1,128]{2,1,0:T(1,128)S(1)}, u32[]{:S(2)}, u32[]{:S(2)}) collective-permute-start(f32[6,1,128]{2,1,0:T(1,128)S(1)} %slice.527), channel_id=1, source_target_pairs={{0,4},{4,8},{8,12},{12,16},{16,20},{20,24},{24,28},{28,32},{32,36}... | collective-permute-start | bytes 9224 | tf_op jit(solution)/shard_map/ppermute | solution.py:12
  7.1 13.7 %collective-permute-start.5 = (f32[6,8,1]{2,1,0:T(8,128)S(1)}, f32[6,8,1]{2,1,0:T(8,128)S(1)}, u32[]{:S(2)}, u32[]{:S(2)}) collective-permute-start(f32[6,8,1]{2,1,0:T(8,128)S(1)} %slice.531), channel_id=1, source_target_pairs={{0,1},{1,2},{2,3},{4,5},{5,6},{6,7},{8,9},{9,10},{10,11},{12,13},{... | collective-permute-start | bytes 584 | tf_op jit(solution)/shard_map/ppermute | solution.py:12
  11.7 14.3 %collective-permute-start.2 = (f32[32,6,8,1]{0,2,3,1:T(8,128)S(1)}, f32[32,6,8,1]{0,2,3,1:T(8,128)S(1)}, u32[]{:S(2)}, u32[]{:S(2)}) collective-permute-start(f32[32,6,8,1]{0,2,3,1:T(8,128)S(1)} %copy.10), channel_id=1, source_target_pairs={{1,0},{2,1},{3,2},{5,4},{6,5},{7,6},{9,8},{10,9},{11,10},{13,12},{... | collective-permute-start | bytes 18440 | tf_op jit(solution)/shard_map/ppermute | solution.py:12
  13.0 13.4 %collective-permute-start = (f32[32,6,1,128]{3,0,2,1:T(8,128)S(1)}, f32[32,6,1,128]{3,0,2,1:T(8,128)S(1)}, u32[]{:S(2)}, u32[]{:S(2)}) collective-permute-start(f32[32,6,1,128]{3,0,2,1:T(8,128)S(1)} %slice.661), channel_id=1, source_target_pairs={{4,0},{8,4},{12,8},{16,12},{20,16},{24,20},{28,24},{32,28},{36,32}... | collective-permute-start | bytes 294920 | tf_op jit(solution)/shard_map/ppermute | solution.py:12
  16.4 0.7 copy-start.25
  17.2 0.7 copy-start.26
  18.6 0.7 copy-start.27
  19.2 0.6 copy-start.23
  20.6 0.7 copy-start.3
  21.5 0.7 copy-start.4
  21.6 3.2 copy-start.7
  22.4 0.7 copy-start.6
  24.7 0.6 copy-start.19
  26.0 1.0 copy-start.5
  27.0 0.7 copy-start.22
  27.8 7.1 %copy-start = (f32[32,6,8,128]{3,0,2,1:T(8,128)}, f32[32,6,8,128]{3,0,2,1:T(8,128)S(1)}, u32[]{:S(2)}) copy-start(f32[32,6,8,128]{3,0,2,1:T(8,128)S(1)} %broadcast_multiply_fusion.5) | copy-start | bytes 2359300
  27.8 2.3 copy-start.21
  27.8 8.3 %collective-permute-start.1 = (f32[32,6,1,128]{3,0,2,1:T(8,128)S(1)}, f32[32,6,1,128]{3,0,2,1:T(8,128)}, u32[]{:S(2)}, u32[]{:S(2)}) collective-permute-start(f32[32,6,1,128]{3,0,2,1:T(8,128)S(1)} %slice.663), channel_id=1, source_target_pairs={{0,4},{4,8},{8,12},{12,16},{16,20},{20,24},{24,28},{28,32},{32,36}... | collective-permute-start | bytes 294920 | tf_op jit(solution)/shard_map/ppermute | solution.py:12
  30.5 4.4 %copy-start.8 = (f32[8,129]{1,0:T(8,128)S(1)}, f32[8,129]{1,0:T(8,128)}, u32[]{:S(2)}) copy-start(f32[8,129]{1,0:T(8,128)} %copy-done.7) | copy-start | bytes 12388
  30.5 4.4 %copy-start.20 = (f32[8,128]{1,0:T(8,128)S(1)}, f32[8,128]{1,0:T(8,128)}, u32[]{:S(2)}) copy-start(f32[8,128]{1,0:T(8,128)} %copy-done.19) | copy-start | bytes 12292
  30.8 4.9 %collective-permute-start.3 = (f32[32,6,8,1]{0,2,3,1:T(8,128)S(1)}, f32[32,6,8,1]{0,2,3,1:T(8,128)S(1)}, u32[]{:S(2)}, u32[]{:S(2)}) collective-permute-start(f32[32,6,8,1]{0,2,3,1:T(8,128)S(1)} %copy.12), channel_id=1, source_target_pairs={{0,1},{1,2},{2,3},{4,5},{5,6},{6,7},{8,9},{9,10},{10,11},{12,13},{... | collective-permute-start | bytes 18440 | tf_op jit(solution)/shard_map/ppermute | solution.py:12
  34.9 1.2 slice-start
  36.1 1.3 copy-start.15
  37.4 0.7 copy-start.13
  37.4 0.7 copy-start.11
  38.8 5.5 %copy-start.24 = (pred[9,128]{1,0:T(8,128)(4,1)S(1)}, pred[9,128]{1,0:T(8,128)(4,1)}, u32[]{:S(2)}) copy-start(pred[9,128]{1,0:T(8,128)(4,1)} %copy-done.23) | copy-start | bytes 3460
  39.2 6.4 %collective-permute-start.7 = (f32[32,6,8,1]{0,2,3,1:T(8,128)S(1)}, f32[32,6,8,1]{0,2,3,1:T(8,128)S(1)}, u32[]{:S(2)}, u32[]{:S(2)}) collective-permute-start(f32[32,6,8,1]{0,2,3,1:T(8,128)S(1)} %copy.14), channel_id=1, source_target_pairs={{1,0},{2,1},{3,2},{5,4},{6,5},{7,6},{9,8},{10,9},{11,10},{13,12},{... | collective-permute-start | bytes 18440 | tf_op jit(solution)/shard_map/ppermute | solution.py:12
  40.5 6.2 %collective-permute-start.6 = (f32[32,6,1,128]{3,0,2,1:T(8,128)S(1)}, f32[32,6,1,128]{3,0,2,1:T(8,128)S(1)}, u32[]{:S(2)}, u32[]{:S(2)}) collective-permute-start(f32[32,6,1,128]{3,0,2,1:T(8,128)S(1)} %slice.781), channel_id=1, source_target_pairs={{4,0},{8,4},{12,8},{16,12},{20,16},{24,20},{28,24},{32,28},{36,32}... | collective-permute-start | bytes 294920 | tf_op jit(solution)/shard_map/ppermute | solution.py:12
  44.4 3.9 copy-start.17
  48.4 10.6 %copy-start.1 = (f32[32,6,8,128]{3,0,2,1:T(8,128)}, f32[32,6,8,128]{3,0,2,1:T(8,128)S(1)}, u32[]{:S(2)}) copy-start(f32[32,6,8,128]{3,0,2,1:T(8,128)S(1)} %broadcast_multiply_fusion.3) | copy-start | bytes 2359300
  48.4 2.8 copy-start.9
  49.1 12.4 %collective-permute-start.8 = (f32[32,6,1,128]{3,0,2,1:T(8,128)}, f32[32,6,1,128]{3,0,2,1:T(8,128)}, u32[]{:S(2)}, u32[]{:S(2)}) collective-permute-start(f32[32,6,1,128]{3,0,2,1:T(8,128)} %slice.784), channel_id=1, source_target_pairs={{0,4},{4,8},{8,12},{12,16},{16,20},{20,24},{24,28},{28,32},{32,36}... | collective-permute-start | bytes 294920 | tf_op jit(solution)/shard_map/ppermute | solution.py:12
  54.6 4.9 %collective-permute-start.9 = (f32[32,6,8,1]{0,2,3,1:T(8,128)}, f32[32,6,8,1]{0,2,3,1:T(8,128)}, u32[]{:S(2)}, u32[]{:S(2)}) collective-permute-start(f32[32,6,8,1]{0,2,3,1:T(8,128)} %copy.16), channel_id=1, source_target_pairs={{0,1},{1,2},{2,3},{4,5},{5,6},{6,7},{8,9},{9,10},{10,11},{12,13},{... | collective-permute-start | bytes 18440 | tf_op jit(solution)/shard_map/ppermute | solution.py:12
  59.0 2.5 slice-start.1
  177.0 0.6 copy-start.28
  177.6 1.4 copy-start.12
  177.6 1.4 copy-start.14
  177.6 1.4 copy-start.16
  278.9 9.0 %collective-permute-start.10 = (f32[32,6,1,128]{3,0,2,1:T(8,128)S(1)}, f32[32,6,1,128]{3,0,2,1:T(8,128)S(1)}, u32[]{:S(2)}, u32[]{:S(2)}) collective-permute-start(f32[32,6,1,128]{3,0,2,1:T(8,128)S(1)} %slice.795), channel_id=1, source_target_pairs={{4,0},{8,4},{12,8},{16,12},{20,16},{24,20},{28,24},{32,28},{36,32}... | collective-permute-start | bytes 294920 | tf_op jit(solution)/shard_map/ppermute | solution.py:12
  281.8 4.8 %collective-permute-start.11 = (f32[32,6,8,1]{0,2,3,1:T(8,128)S(1)}, f32[32,6,8,1]{0,2,3,1:T(8,128)S(1)}, u32[]{:S(2)}, u32[]{:S(2)}) collective-permute-start(f32[32,6,8,1]{0,2,3,1:T(8,128)S(1)} %copy.18), channel_id=1, source_target_pairs={{1,0},{2,1},{3,2},{5,4},{6,5},{7,6},{9,8},{10,9},{11,10},{13,12},{... | collective-permute-start | bytes 18440 | tf_op jit(solution)/shard_map/ppermute | solution.py:12
  287.9 1.8 copy-start.10
  289.7 0.7 copy-start.18
  290.5 0.9 copy-start.2
  291.4 13.3 %collective-permute-start.12 = (f32[32,6,1,128]{3,0,2,1:T(8,128)}, f32[32,6,1,128]{3,0,2,1:T(8,128)}, u32[]{:S(2)}, u32[]{:S(2)}) collective-permute-start(f32[32,6,1,128]{3,0,2,1:T(8,128)} %slice.798), channel_id=1, source_target_pairs={{0,4},{4,8},{8,12},{12,16},{16,20},{20,24},{24,28},{28,32},{32,36}... | collective-permute-start | bytes 294920 | tf_op jit(solution)/shard_map/ppermute | solution.py:12
  298.6 4.9 %collective-permute-start.13 = (f32[32,6,8,1]{0,2,3,1:T(8,128)S(1)}, f32[32,6,8,1]{0,2,3,1:T(8,128)S(1)}, u32[]{:S(2)}, u32[]{:S(2)}) collective-permute-start(f32[32,6,8,1]{0,2,3,1:T(8,128)S(1)} %copy.20), channel_id=1, source_target_pairs={{0,1},{1,2},{2,3},{4,5},{5,6},{6,7},{8,9},{9,10},{10,11},{12,13},{... | collective-permute-start | bytes 18440 | tf_op jit(solution)/shard_map/ppermute | solution.py:12
  408.1 0.7 copy-start.29
where the time goes:
time: 415 us; the launch traced here: 413 us
  blocking collectives  312 us (75%)
  starting transfers between devices  41.7 us (10%)
  local copies, waits for them, and re-layouts  31.7 us (8%)
  other arithmetic  21.5 us (5%)
  waiting for transfers between devices  4.56 us (1%)
    psum x2, blocking collectives, inner_rz(): return lax.psum(jnp.sum(first * second, axis=(1, 2, 3)), ('slab', 'sub'))  212 us
    psum x1, blocking collectives, inner_pq(): return lax.psum(jnp.sum(first * second, axis=(1, 2, 3)), ('slab', 'sub'))  101 us
    ppermute x14, starting transfers between devices, from_behind(): lax.ppermute(value, axis, [(source, source + steps) for source in range(i...  41.7 us
    unnamed x64, local copies, waits for them, and re-layouts  10.6 us
  transfers between devices with their start and end apart: 14, of which 4 were waited for; matrix products, arithmetic and copies ran while one was open for 6% of the time, Pallas kernels for 0%

commit v1 on v0

--- a/solution.py
+++ b/solution.py
@@ -83,7 +83,7 @@
 
 
 def inner_pq(first, second):
-    return lax.psum(jnp.sum(first * second, axis=(1, 2, 3)), ("slab", "sub"))
+    return lax.psum(lax.psum(jnp.sum(first * second, axis=(1, 2, 3)), "slab"), "sub")
 
 
 def body(mode_shapes, span_stiff, chord_stiff, span_geo, chord_geo, ground, chord_len):

time: 415 us -> 820 us (1.98)
  blocking collectives: 312 us -> 717 us
    psum x1 -> x4, blocking collectives: 101 us -> 516 us  [the longest x2 498 us: inner_pq(): lax.psum(jnp.sum(first * second, axis=(1, 2, 3)), 'slab')]
    psum x2, blocking collectives: 212 us -> 202 us  [inner_rz(): return lax.psum(jnp.sum(first * second, axis=(1, 2, 3)), ('slab', 'sub'))]
  transfers between devices with their start and end apart: 14 -> 14, of which waited for: 4 -> 4; matrix products, arithmetic and copies ran while one was open for 6% -> 3% of each run, Pallas kernels for 0% -> 0%
where the time goes in v1:
time: 820 us; the launch traced here: 818 us
  blocking collectives  717 us (87%)
  starting transfers between devices  41.3 us (5%)
  local copies, waits for them, and re-layouts  31.6 us (4%)
  other arithmetic  21.5 us (3%)
    psum x2, blocking collectives, inner_pq(): lax.psum(jnp.sum(first * second, axis=(1, 2, 3)), 'slab')  498 us
    psum x2, blocking collectives, inner_rz(): return lax.psum(jnp.sum(first * second, axis=(1, 2, 3)), ('slab', 'sub'))  202 us
    ppermute x14, starting transfers between devices, from_behind(): lax.ppermute(value, axis, [(source, source + steps) for source in range(i...  41.3 us
    psum x2, blocking collectives, inner_pq(): lax.psum(lax.psum(jnp.sum(first * second, axis=(1, 2, 3)), 'slab'), 'sub')  17.5 us
  transfers between devices with their start and end apart: 14, of which 4 were waited for; matrix products, arithmetic and copies ran while one was open for 3% of the time, Pallas kernels for 0%

profile of v1, /device:TPU:1, one launch (start us, length us, event | category | flops | bytes accessed | tf_op | source)
XLA Modules:
  0.0 817.7 jit_solution(14137330776508560358)
XLA Ops:
  0.6 0.7 slice.527
  1.4 4.9 collective-permute-start.4
  6.3 0.8 slice.531
  7.1 3.1 collective-permute-start.5
  10.2 1.1 copy_convert_fusion
  11.7 1.3 collective-permute-start.2
  13.0 3.3 collective-permute-start
  16.4 0.7 copy-done.25
  17.9 0.7 slice_select_fusion
  18.6 0.6 copy-done.27
  19.3 0.6 slice_select_fusion.1
  19.9 0.7 slice_convert_fusion
  21.6 0.6 copy-done.4
  22.5 0.7 copy-done.6
  23.4 0.7 fusion.94
  24.1 0.7 fusion.78
  24.7 0.6 copy-done.19
  25.3 0.7 fusion.70
  26.3 0.6 copy-done.5
  27.8 2.2 collective-permute-start.1
  30.8 4.0 collective-permute-start.3
  34.9 0.9 collective-permute-done.3
  36.1 1.3 fusion.3
  37.4 0.6 copy-done.13
  39.2 1.3 collective-permute-start.7
  40.5 3.8 collective-permute-start.6
  44.3 0.9 slice.780
  45.9 0.8 collective-permute-done.6
  46.7 1.6 fusion.9
  48.4 0.7 slice.784
  49.1 2.1 collective-permute-start.8
  51.3 1.2 slice.786
  52.5 2.1 copy.16
  54.6 4.4 collective-permute-start.9
  59.0 0.5 collective-permute-done.9
  59.5 2.0 copy.17
  61.5 2.6 multiply_reduce_fusion.2
  64.1 252.7 %psum.43 = f32[32]{0:T(128)S(1)} all-reduce(f32[32]{0:T(128)S(1)} %get-tuple-element.6), channel_id=1, replica_groups=mesh['slab'=128,'sub'=4] {'slab'}, use_global_device_ids=true, to_apply=%region_7.0 | all-reduce | flops 32 | bytes 256 | tf_op jit(solution)/shard_map/psum | solution.py:86
  316.8 10.0 %psum.44 = f32[32]{0:T(128)S(1)} all-reduce(f32[32]{0:T(128)S(1)} %psum.43), channel_id=1, replica_groups=mesh['slab'=128,'sub'=4] {'sub'}, use_global_device_ids=true, to_apply=%region_8.0 | all-reduce | flops 32 | bytes 256 | tf_op jit(solution)/shard_map/psum | solution.py:86
  326.8 101.1 %psum.42 = f32[32]{0:T(128)S(1)} all-reduce(f32[32]{0:T(128)S(1)} %get-tuple-element.7), channel_id=1, replica_groups=mesh['slab'=128,'sub'=4] {'slab','sub'}, use_global_device_ids=true, to_apply=%region_3.0 | all-reduce | flops 32 | bytes 256 | tf_op jit(solution)/shard_map/psum | solution.py:82
  427.9 0.5 copy-done.28
  428.5 1.3 multiply_subtract_fusion.1
  430.8 100.5 %psum.45 = f32[32]{0:T(128)S(1)} all-reduce(f32[32]{0:T(128)S(1)} %multiply_reduce_fusion.1), channel_id=1, replica_groups=mesh['slab'=128,'sub'=4] {'slab','sub'}, use_global_device_ids=true, to_apply=%region_10.0 | all-reduce | flops 32 | bytes 256 | tf_op jit(solution)/shard_map/psum | solution.py:82
  531.6 2.6 collective-permute-start.10
  534.5 1.3 collective-permute-start.11
  535.8 0.9 slice.794
  537.0 2.3 collective-permute-done.11
  539.3 1.2 copy.19
  540.6 1.8 fusion.14
  542.4 0.7 copy-done.18
  543.2 0.7 slice.798
  544.1 3.9 collective-permute-start.12
  548.1 1.2 slice.800
  549.2 1.5 copy.20
  550.7 3.0 collective-permute-start.13
  553.7 2.0 slice.799
  555.8 1.2 copy.21
  557.0 2.7 multiply_reduce_fusion
  559.8 245.6 %psum.46 = f32[32]{0:T(128)S(1)} all-reduce(f32[32]{0:T(128)S(1)} %get-tuple-element.12), channel_id=1, replica_groups=mesh['slab'=128,'sub'=4] {'slab'}, use_global_device_ids=true, to_apply=%region_14.0 | all-reduce | flops 32 | bytes 256 | tf_op jit(solution)/shard_map/psum | solution.py:86
  805.4 7.5 psum.47
  812.8 0.6 copy-done.29
  813.5 1.5 multiply_subtract_fusion
  815.0 1.3 copy.23
  816.4 1.3 copy.22
  (130 shorter events, 9.2 us)
Async XLA Ops:
  1.4 20.2 %collective-permute-start.4 = (f32[6,1,128]{2,1,0:T(1,128)S(1)}, f32[6,1,128]{2,1,0:T(1,128)S(1)}, u32[]{:S(2)}, u32[]{:S(2)}) collective-permute-start(f32[6,1,128]{2,1,0:T(1,128)S(1)} %slice.527), channel_id=1, source_target_pairs={{0,4},{4,8},{8,12},{12,16},{16,20},{20,24},{24,28},{28,32},{32,36}... | collective-permute-start | bytes 9224 | tf_op jit(solution)/shard_map/ppermute | solution.py:12
  7.1 13.7 %collective-permute-start.5 = (f32[6,8,1]{2,1,0:T(8,128)S(1)}, f32[6,8,1]{2,1,0:T(8,128)S(1)}, u32[]{:S(2)}, u32[]{:S(2)}) collective-permute-start(f32[6,8,1]{2,1,0:T(8,128)S(1)} %slice.531), channel_id=1, source_target_pairs={{0,1},{1,2},{2,3},{4,5},{5,6},{6,7},{8,9},{9,10},{10,11},{12,13},{... | collective-permute-start | bytes 584 | tf_op jit(solution)/shard_map/ppermute | solution.py:12
  11.7 14.3 %collective-permute-start.2 = (f32[32,6,8,1]{0,2,3,1:T(8,128)S(1)}, f32[32,6,8,1]{0,2,3,1:T(8,128)S(1)}, u32[]{:S(2)}, u32[]{:S(2)}) collective-permute-start(f32[32,6,8,1]{0,2,3,1:T(8,128)S(1)} %copy.10), channel_id=1, source_target_pairs={{1,0},{2,1},{3,2},{5,4},{6,5},{7,6},{9,8},{10,9},{11,10},{13,12},{... | collective-permute-start | bytes 18440 | tf_op jit(solution)/shard_map/ppermute | solution.py:12
  13.0 13.3 %collective-permute-start = (f32[32,6,1,128]{3,0,2,1:T(8,128)S(1)}, f32[32,6,1,128]{3,0,2,1:T(8,128)S(1)}, u32[]{:S(2)}, u32[]{:S(2)}) collective-permute-start(f32[32,6,1,128]{3,0,2,1:T(8,128)S(1)} %slice.661), channel_id=1, source_target_pairs={{4,0},{8,4},{12,8},{16,12},{20,16},{24,20},{28,24},{32,28},{36,32}... | collective-permute-start | bytes 294920 | tf_op jit(solution)/shard_map/ppermute | solution.py:12
  16.4 0.7 copy-start.25
  17.2 0.7 copy-start.26
  18.6 0.7 copy-start.27
  19.3 0.6 copy-start.23
  20.6 0.7 copy-start.3
  21.5 0.7 copy-start.4
  21.6 3.2 copy-start.7
  22.5 0.7 copy-start.6
  24.7 0.6 copy-start.19
  26.0 1.0 copy-start.5
  27.0 0.7 copy-start.22
  27.8 7.1 copy-start
  27.8 2.3 copy-start.21
  27.8 8.3 %collective-permute-start.1 = (f32[32,6,1,128]{3,0,2,1:T(8,128)S(1)}, f32[32,6,1,128]{3,0,2,1:T(8,128)}, u32[]{:S(2)}, u32[]{:S(2)}) collective-permute-start(f32[32,6,1,128]{3,0,2,1:T(8,128)S(1)} %slice.663), channel_id=1, source_target_pairs={{0,4},{4,8},{8,12},{12,16},{16,20},{20,24},{24,28},{28,32},{32,36}... | collective-permute-start | bytes 294920 | tf_op jit(solution)/shard_map/ppermute | solution.py:12
  30.5 4.4 copy-start.8
  30.5 4.4 copy-start.20
  30.8 4.9 collective-permute-start.3
  34.9 1.2 slice-start
  36.1 1.3 copy-start.15
  37.4 0.7 copy-start.13
  37.4 0.7 copy-start.11
  38.8 5.5 copy-start.24
  39.2 6.4 collective-permute-start.7
  40.5 6.2 collective-permute-start.6
  44.3 3.9 copy-start.17
  48.4 10.6 %copy-start.1 = (f32[32,6,8,128]{3,0,2,1:T(8,128)}, f32[32,6,8,128]{3,0,2,1:T(8,128)S(1)}, u32[]{:S(2)}) copy-start(f32[32,6,8,128]{3,0,2,1:T(8,128)S(1)} %broadcast_multiply_fusion.3) | copy-start | bytes 2359300
  48.4 2.8 copy-start.9
  49.1 12.4 %collective-permute-start.8 = (f32[32,6,1,128]{3,0,2,1:T(8,128)}, f32[32,6,1,128]{3,0,2,1:T(8,128)}, u32[]{:S(2)}, u32[]{:S(2)}) collective-permute-start(f32[32,6,1,128]{3,0,2,1:T(8,128)} %slice.784), channel_id=1, source_target_pairs={{0,4},{4,8},{8,12},{12,16},{16,20},{20,24},{24,28},{28,32},{32,36}... | collective-permute-start | bytes 294920 | tf_op jit(solution)/shard_map/ppermute | solution.py:12
  54.6 4.9 collective-permute-start.9
  59.0 2.5 slice-start.1
  427.9 0.5 copy-start.28
  428.5 1.4 copy-start.12
  428.5 1.4 copy-start.14
  428.5 1.4 copy-start.16
  531.6 9.0 %collective-permute-start.10 = (f32[32,6,1,128]{3,0,2,1:T(8,128)S(1)}, f32[32,6,1,128]{3,0,2,1:T(8,128)S(1)}, u32[]{:S(2)}, u32[]{:S(2)}) collective-permute-start(f32[32,6,1,128]{3,0,2,1:T(8,128)S(1)} %slice.795), channel_id=1, source_target_pairs={{4,0},{8,4},{12,8},{16,12},{20,16},{24,20},{28,24},{32,28},{36,32}... | collective-permute-start | bytes 294920 | tf_op jit(solution)/shard_map/ppermute | solution.py:12
  534.5 4.8 collective-permute-start.11
  540.6 1.8 copy-start.10
  542.4 0.7 copy-start.18
  543.2 0.9 copy-start.2
  544.1 12.9 %collective-permute-start.12 = (f32[32,6,1,128]{3,0,2,1:T(8,128)}, f32[32,6,1,128]{3,0,2,1:T(8,128)}, u32[]{:S(2)}, u32[]{:S(2)}) collective-permute-start(f32[32,6,1,128]{3,0,2,1:T(8,128)} %slice.798), channel_id=1, source_target_pairs={{0,4},{4,8},{8,12},{12,16},{16,20},{20,24},{24,28},{28,32},{32,36}... | collective-permute-start | bytes 294920 | tf_op jit(solution)/shard_map/ppermute | solution.py:12
  550.7 5.1 collective-permute-start.13
  812.8 0.6 copy-start.29
